TPU v7x, 256 devices: a whole 4x4x8 slice. The times are simulated.
256 devices in a mesh: item: 64 (over z, y, core), dp: 4 (over x).
Axes of the slice: x: 4, y: 4, z: 8, core: 2. Of those that a mesh axis runs over, the one named last changes fastest.
Arguments:
- query_feats: bfloat16 [4, 1024, 256], P('dp', 'item'), may hold values from -6 to 6
- positives: int32 [4, 1024], P('dp'), may hold values from 0 to 262143
- query_count: int32 [4, 64], P('dp'), may hold values from 1 to 16, as said below
- item_table: bfloat16 [262144, 256], P('item'), may hold values from -6 to 6
- item_gates: float32 [4, 262144], P(None, 'item'), may hold values from -5 to 5
- w_in: bfloat16 [256, 512], replicated, may hold values from -0.375 to 0.375
- w_out: bfloat16 [512, 256], replicated, may hold values from -0.25 to 0.25
- w_gate: bfloat16 [512, 4], replicated, may hold values from -1.25 to 1.25
Outputs:
- grad_feats: float32 [4, 1024, 256], P('dp', 'item')
- grad_w_in: float32 [256, 512], replicated
- grad_w_out: float32 [512, 256], replicated
- grad_w_gate: float32 [512, 4], replicated
Inputs may be any that keep to these rules, and one draw needn't show every extreme that they name: `query_count`: valid queries of a device's slots; the counts of one group sum to at most 768, exactly that in some group, and some device of every group has all 16 slots valid.
All inputs are finite; a program needn't handle non-finite values.
Results may differ from a plain program's by a relative error of at most 0.0053.
Values may be sent and summed in bfloat16 or wider, within the bound.
A program may use at most 64 MiB of HBM per device.

v0:
```python
import jax
import jax.numpy as jnp
from jax import lax
from jax.sharding import PartitionSpec as P

EPS = 1e-06
TAU = 0.05


def unit_rows(raw_vals):
    scale = lax.rsqrt(jnp.sum(raw_vals * raw_vals, axis=-1, keepdims=True) + EPS)
    return (raw_vals * scale, scale)


def gate_weights(gate_logits, reduce_axis):
    exp_terms = jnp.exp(gate_logits)
    return exp_terms / jnp.sum(exp_terms, axis=reduce_axis, keepdims=True)


def item_sweep(query_rows, query_gate, item_norm, item_gates):
    row_count = query_rows.shape[0]
    components = query_rows.shape[1]
    comp_width = query_rows.shape[2]
    item_span = item_norm.shape[0]
    block_len = min(512, item_span)
    block_count = item_span // block_len
    item_blocks = item_norm.reshape(block_count, block_len, components, comp_width)
    gate_blocks = item_gates.reshape(components, block_count, block_len).transpose(1, 0, 2)
    gate_f = query_gate.astype(jnp.float32).T[:, :, None]

    def one_block(state_in, input_block_part):
        totals, update_delta, gate_sum = state_in
        item_part, gate_part = input_block_part
        score_matrix = jnp.einsum(
            "rkd,ikd->kri", query_rows, item_part, preferred_element_type=jnp.float32
        )
        weights = gate_weights(gate_f + gate_part[:, None, :], 0)
        logits = jnp.sum(weights * score_matrix, axis=0) / TAU
        exp_logit = jnp.exp(logits)
        totals = totals + jnp.sum(exp_logit, axis=1)
        coef_bf = (exp_logit[None] * weights / TAU).astype(jnp.bfloat16)
        update_delta = update_delta + jnp.einsum(
            "kri,ikd->rkd", coef_bf, item_part, preferred_element_type=jnp.float32
        )
        gate_sum = (
            gate_sum
            + jnp.sum(exp_logit[None] * weights * (score_matrix - TAU * logits[None]), axis=2) / TAU
        )
        return ((totals, update_delta, gate_sum), None)

    initial = (
        jnp.zeros((row_count,), jnp.float32),
        jnp.zeros((row_count, components, comp_width), jnp.float32),
        jnp.zeros((components, row_count), jnp.float32),
    )
    (totals, update_delta, gate_sum), _ = lax.scan(one_block, initial, (item_blocks, gate_blocks))
    return (totals, update_delta, gate_sum.T)


def positive_terms(query_rows, query_gate, positive, item_norm, item_gates, item_base):
    item_span = item_norm.shape[0]
    local_id = positive - item_base
    inside = (local_id >= 0) & (local_id < item_span)
    safe_id = jnp.clip(local_id, 0, item_span - 1)
    item_pos = jnp.take(item_norm, safe_id, axis=0).astype(jnp.float32)
    gate_pos = jnp.take(item_gates, safe_id, axis=1).T
    query_float_rows = query_rows.astype(jnp.float32)
    score_pos = jnp.sum(query_float_rows * item_pos, axis=-1)
    weight_pos = gate_weights(query_gate.astype(jnp.float32) + gate_pos, 1)
    logit_pos = jnp.sum(weight_pos * score_pos, axis=-1) / TAU
    keep_rows = inside.astype(jnp.float32)
    pos_query = weight_pos[:, :, None] * item_pos / TAU * keep_rows[:, None, None]
    pos_gate = weight_pos * (score_pos - TAU * logit_pos[:, None]) / TAU * keep_rows[:, None]
    return (pos_query, pos_gate)


def per_device(query_feats, positives, query_count, item_table, item_gates, w_in, w_out, w_gate):
    shard_count = lax.axis_size("item")
    item_rank = lax.axis_index("item")
    own_rows = query_feats.shape[1]
    feat_width = query_feats.shape[2]
    components = w_gate.shape[1]
    emb_width = w_out.shape[1]
    comp_width = emb_width // components
    slot_total = own_rows * shard_count
    features = query_feats[0]
    counts = query_count[0]
    preact = jnp.dot(features, w_in, preferred_element_type=jnp.float32)
    hidden = jax.nn.silu(preact).astype(jnp.bfloat16)
    query_raw = jnp.dot(hidden, w_out, preferred_element_type=jnp.float32).reshape(
        own_rows, components, comp_width
    )
    query_gate = jnp.dot(hidden, w_gate, preferred_element_type=jnp.float32).astype(jnp.bfloat16)
    query_unit, query_scale = unit_rows(query_raw)
    query_norm = query_unit.astype(jnp.bfloat16).reshape(own_rows, emb_width)
    all_query, all_gate = (
        lax.all_gather(query_norm, "item", axis=0, tiled=True),
        lax.all_gather(query_gate, "item", axis=0, tiled=True),
    )
    item_span = item_table.shape[0]
    item_norm = unit_rows(
        item_table.astype(jnp.float32).reshape(item_span, components, comp_width)
    )[0].astype(jnp.bfloat16)
    slot_in_dev = jnp.arange(own_rows, dtype=jnp.int32)
    valid_slot = (slot_in_dev[None, :] < counts[:, None]).reshape(slot_total)
    item_base = item_rank * item_span
    group_position = positives[0]
    query_rows = all_query.reshape(-1, components, comp_width)
    totals, update_delta, gate_sum = item_sweep(query_rows, all_gate, item_norm, item_gates)
    pos_query, pos_gate = positive_terms(
        query_rows, all_gate, group_position, item_norm, item_gates, item_base
    )
    live_f = valid_slot.astype(jnp.float32)
    totals_all = lax.psum(totals, "item")
    query_term_part = (update_delta / totals_all[:, None, None] - pos_query) * live_f[:, None, None]
    term_gate = (gate_sum / totals_all[:, None] - pos_gate) * live_f[:, None]
    grad_query, grad_gate = (
        lax.psum_scatter(
            query_term_part.reshape(slot_total, emb_width), "item", scatter_dimension=0, tiled=True
        ),
        lax.psum_scatter(term_gate, "item", scatter_dimension=0, tiled=True),
    )
    grad_query = grad_query.reshape(own_rows, components, comp_width)
    dot_sum = jnp.sum(grad_query * query_raw, axis=-1, keepdims=True)
    grad_raw = (query_scale * grad_query - query_raw * query_scale**3 * dot_sum).reshape(
        own_rows, emb_width
    )
    highest = lax.Precision.HIGHEST
    grad_hidden = jnp.dot(grad_raw, w_out.astype(jnp.float32).T, precision=highest) + jnp.dot(
        grad_gate, w_gate.astype(jnp.float32).T, precision=highest
    )
    sigmoid_pre = jax.nn.sigmoid(preact)
    grad_preact = grad_hidden * sigmoid_pre * (1.0 + preact * (1.0 - sigmoid_pre))
    grad_feats = jnp.dot(grad_preact, w_in.astype(jnp.float32).T, precision=highest).reshape(
        1, own_rows, feat_width
    )
    hidden_f = hidden.astype(jnp.float32)
    part_in = jnp.dot(features.astype(jnp.float32).T, grad_preact, precision=highest)
    part_out = jnp.dot(hidden_f.T, grad_raw, precision=highest)
    part_gate = jnp.dot(hidden_f.T, grad_gate, precision=highest)
    grad_w_in, grad_w_out, grad_w_gate = lax.psum((part_in, part_out, part_gate), ("item", "dp"))
    return (grad_feats, grad_w_in, grad_w_out, grad_w_gate)


def solution(mesh):
    in_specs = (
        P("dp", "item", None),
        P("dp", None),
        P("dp", None),
        P("item", None),
        P(None, "item"),
        P(),
        P(),
        P(),
    )
    out_specs = (P("dp", "item", None), P(), P(), P())
    return jax.shard_map(
        per_device, mesh=mesh, in_specs=in_specs, out_specs=out_specs, check_vma=False
    )
```

profile of v0, /device:TPU:2, one launch (start us, length us, event | category | flops | bytes accessed | tf_op | source)
XLA Modules:
  0.0 914.7 jit_solution(16929554966947675786)
XLA Ops:
  16.9 53.5 %all_gather.7 = bf16[1024,256]{1,0:T(8,128)(2,1)S(1)} all-gather(bf16[16,256]{1,0:T(8,128)(2,1)S(1)} %multiply_convert_fusion.9), channel_id=1, replica_groups=mesh['item'=64,'dp'=4] {'item'}, dimensions={0}, use_global_device_ids=true | all-gather | bytes 532480 | tf_op jit(solution)/shard_map/all_gather | solution.py:97
  73.4 7.0 copy.75
  80.4 5.7 gather_fusion.1
  87.5 42.9 %all-gather = bf16[64,16,4]{1,2,0:T(4,128)(2,1)S(1)} all-gather(bf16[1,16,4]{1,2,0:T(4,128)(2,1)S(1)} %fusion.19), channel_id=1, replica_groups=mesh['item'=64,'dp'=4] {'item'}, dimensions={0}, use_global_device_ids=true | all-gather | bytes 8320 | tf_op jit(solution)/shard_map/all_gather | solution.py:98
  132.1 4.4 gather_fusion
  137.7 6.0 copy.81
  147.2 118.4 %while.17 = (s32[]{:T(128)}, f32[1024]{0:T(1024)S(1)}, f32[1024,4,64]{0,2,1:T(8,128)}, f32[4,1024]{1,0:T(4,128)S(1)}, f32[4,1024,1]{1,0,2:T(4,128)S(1)}, /*index...) while((s32[]{:T(128)}, f32[1024]{0:T(1024)S(1)}, ...), condition=%wide.region_7.8_spmd.clone, body=%wide.region_2.7_spmd.clone.sunk | while | flops 573056000 | bytes 49480844 | solution.py:56
  149.4 4.1 fusion.63
  156.8 5.0 fusion.64
  164.0 4.1 fusion.63
  171.4 5.3 fusion.64
  178.8 4.1 fusion.63
  186.2 5.3 fusion.64
  201.1 5.3 fusion.64
  208.4 4.1 fusion.63
  215.9 5.3 fusion.64
  230.7 5.3 fusion.64
  238.1 4.1 fusion.63
  245.5 5.3 fusion.64
  260.4 5.3 fusion.64
  265.7 126.8 %psum.28 = f32[1024]{0:T(1024)S(1)} all-reduce(f32[1024]{0:T(1024)S(1)} %get-tuple-element.108), channel_id=1, replica_groups=mesh['item'=64,'dp'=4] {'item'}, use_global_device_ids=true, to_apply=%region_8.9 | all-reduce | flops 1024 | bytes 8192 | tf_op jit(solution)/shard_map/psum | solution.py:114
  398.0 249.1 %all-reduce = f32[1024,4]{1,0:T(8,128)S(1)} all-reduce(f32[1024,4]{1,0:T(8,128)S(1)} %copy.78), channel_id=3, replica_groups=mesh['item'=64,'dp'=4] {'item'}, use_global_device_ids=true, to_apply=%region_14.15.clone | all-reduce | flops 4096 | bytes 32768
  652.1 71.6 %psum.31 = f32[512,4]{0,1:T(4,128)} all-reduce(f32[512,4]{0,1:T(4,128)S(1)} %fusion.30), channel_id=1, replica_groups=mesh['item'=64,'dp'=4] {'item','dp'}, use_global_device_ids=true, to_apply=%region_17.18 | all-reduce | flops 2048 | bytes 16384 | tf_op jit(solution)/shard_map/psum | solution.py:141
  724.6 179.4 %all-reduce.4.cloned.1.call-done = (f32[256,512]{0,1:T(8,128)}, f32[512,256]{1,0:T(8,128)}) async-done(((f32[256,512]{0,1:T(8,128)}, f32[512,256]{1,0:T(8,128)}), (f32[256,512]{0,1:T(8,128)}, f32[512,256]{1,0:T(8,128)})) %all-reduce.4.cloned.1.call-update) | async-done | bytes 1048592 | tf_op jit(solution)/shard_map/psum | solution.py:141
  (169 shorter events, 90.9 us)
Async XLA Ops:
  7.2 7.3 copy-start
  7.2 639.9 %reduce-scatter.2.cloned.1.call-start = ((), (), s32[]{:S(2)}) async-start(), calls=%async_computation.1 | async-start | bytes 1064960 | tf_op jit(solution)/shard_map/reduce_scatter | solution.py:118
  10.2 5.0 copy-start.2
  73.4 13.9 %copy-start.18 = (bf16[512,4]{0,1:T(4,128)(2,1)S(1)}, bf16[512,4]{0,1:T(4,128)(2,1)}, u32[]{:S(2)}) copy-start(bf16[512,4]{0,1:T(4,128)(2,1)} %param.17) | copy-start | bytes 12292
  80.4 7.1 copy-start.10
  137.7 8.9 copy-start.5
  147.2 245.3 %copy-start.17 = (s32[1,64]{1,0:T(1,128)S(1)}, s32[1,64]{1,0:T(1,128)}, u32[]{:S(2)}) copy-start(s32[1,64]{1,0:T(1,128)} %param.12) | copy-start | bytes 772
  147.2 245.4 %copy-start.6 = (f32[1024,4]{0,1:T(4,128)S(1)}, f32[1024,4]{0,1:T(4,128)}, u32[]{:S(2)}) copy-start(f32[1024,4]{0,1:T(4,128)} %copy-done.5) | copy-start | bytes 49156
  149.4 4.4 copy-start.1
  163.9 4.4 copy-start.1
  178.8 4.4 copy-start.1
  193.6 4.4 copy-start.1
  208.4 4.4 copy-start.1
  238.1 4.4 copy-start.1
  252.9 4.4 copy-start.1
  265.6 130.7 %copy-start.9 = (f32[1,1024]{1,0:T(1,128)S(1)}, f32[1,1024]{1,0:T(1,128)}, u32[]{:S(2)}) copy-start(f32[1,1024]{1,0:T(1,128)} %and_select_fusion) | copy-start | bytes 12292
  265.6 130.9 %copy-start.14 = (f32[16,4]{1,0:T(8,128)S(1)}, f32[16,4]{1,0:T(8,128)}, u32[]{:S(2)}) copy-start(f32[16,4]{1,0:T(8,128)} %get-tuple-element.223) | copy-start | bytes 772
  265.7 131.1 %copy-start.20 = (u32[256]{0:T(256)S(1)}, u32[256]{0:T(256)}, u32[]{:S(2)}) copy-start(u32[256]{0:T(256)} %constant.108) | copy-start | bytes 3076
  265.7 382.5 %copy-start.8 = (f32[16,256]{1,0:T(8,128)S(1)}, f32[16,256]{1,0:T(8,128)}, u32[]{:S(2)}) copy-start(f32[16,256]{1,0:T(8,128)} %copy-done.7) | copy-start | bytes 49156
  265.7 383.3 %copy-start.3 = (bf16[512,256]{1,0:T(8,128)(2,1)S(1)}, bf16[512,256]{1,0:T(8,128)(2,1)}, u32[]{:S(2)}) copy-start(bf16[512,256]{1,0:T(8,128)(2,1)} %param.16) | copy-start | bytes 786436
  393.4 257.1 %copy-start.13 = (f32[16,512]{1,0:T(8,128)S(1)}, f32[16,512]{1,0:T(8,128)}, u32[]{:S(2)}) copy-start(f32[16,512]{1,0:T(8,128)} %get-tuple-element.226) | copy-start | bytes 98308
  393.4 257.1 %copy-start.19 = (bf16[512,4]{0,1:T(4,128)(2,1)S(1)}, bf16[512,4]{0,1:T(4,128)(2,1)}, u32[]{:S(2)}) copy-start(bf16[512,4]{0,1:T(4,128)(2,1)} %param.17) | copy-start | bytes 12292
  393.4 257.2 %copy-start.12 = (bf16[1,16,256]{2,1,0:T(8,128)(2,1)S(1)}, bf16[1,16,256]{2,1,0:T(8,128)(2,1)}, u32[]{:S(2)}) copy-start(bf16[1,16,256]{2,1,0:T(8,128)(2,1)} %param.10) | copy-start | bytes 24580
  396.2 507.7 %all-reduce.4.cloned.1.call-start = ((), (), s32[]{:S(2)}) async-start(), calls=%async_computation.2 | async-start | bytes 2097152 | tf_op jit(solution)/shard_map/psum | solution.py:141
  (6 other events, 18.4 us)
Sparse Core Ops, SparseCore 0:
  396.4 134.9 reduce-scatter.1
  652.0 251.9 all-reduce.3
where the time goes:
time: 916 us; the launch traced here: 915 us
  blocking collectives  544 us (59%)
  waiting for transfers between devices  179 us (20%)
  matrix products  79.4 us (9%)
  other arithmetic  51.6 us (6%)
  local copies, waits for them, and re-layouts  45 us (5%)
  between operations  15 us (2%)
    unnamed x1, blocking collectives  249 us
    psum x1, waiting for transfers between devices, per_device(): lax.psum((part_in, part_out, part_gate), ('item', 'dp'))  179 us
    psum x1, blocking collectives, per_device(): totals_all = lax.psum(totals, 'item')  127 us
    psum x1, blocking collectives, per_device(): lax.psum((part_in, part_out, part_gate), ('item', 'dp'))  71.6 us
    all_gather x1, blocking collectives, per_device(): lax.all_gather(query_norm, 'item', axis=0, tiled=True)  53.5 us
    all_gather x1, blocking collectives, per_device(): lax.all_gather(query_gate, 'item', axis=0, tiled=True)  42.9 us
    dot_general x8, matrix products, one_block(): jnp.einsum('kri,ikd->rkd', coef_bf, item_part, preferred_element_type=jnp...  41.9 us
    dot_general x8, matrix products, one_block(): jnp.einsum('rkd,ikd->kri', query_rows, item_part, preferred_element_type=...  32.5 us
  transfers between devices with their start and end apart: 2, of which 1 were waited for; matrix products, arithmetic and copies ran while one was open for 0% of the time, Pallas kernels for 0%

commit v1 on v0

--- a/solution.py
+++ b/solution.py
@@ -94,7 +94,9 @@
     query_unit, query_scale = unit_rows(query_raw)
     query_norm = query_unit.astype(jnp.bfloat16).reshape(own_rows, emb_width)
     all_query, all_gate = (
-        lax.all_gather(query_norm, "item", axis=0, tiled=True),
+        jnp.concatenate(
+            lax.all_to_all(jnp.stack([query_norm] * lax.axis_size("item")), "item", 0, 0), axis=0
+        ),
         lax.all_gather(query_gate, "item", axis=0, tiled=True),
     )
     item_span = item_table.shape[0]

time: 916 us -> 879 us (0.960)
  blocking collectives: 544 us -> 492 us
  starting transfers between devices: 0.08 us -> 12.2 us
    all_gather x1 -> x0, blocking collectives: 53.5 us -> none  [per_device(): lax.all_gather(query_norm, 'item', axis=0, tiled=True)]
    all_to_all x0 -> x1, starting transfers between devices: none -> 12.1 us  [per_device(): lax.all_to_all(jnp.stack([query_norm] * lax.axis_size('item')), 'item', 0...]
    unnamed x48 -> x43, local copies, waits for them, and re-layouts: 17.7 us -> 18.6 us
  transfers between devices with their start and end apart: 2 -> 3, of which waited for: 1 -> 1; matrix products, arithmetic and copies ran while one was open for 0% -> 5% of each run, Pallas kernels for 0% -> 0%
where the time goes in v1:
time: 879 us; the launch traced here: 878 us
  blocking collectives  492 us (56%)
  waiting for transfers between devices  181 us (21%)
  matrix products  81 us (9%)
  other arithmetic  48.9 us (6%)
  local copies, waits for them, and re-layouts  46.6 us (5%)
  between operations  15.1 us (2%)
  starting transfers between devices  12.2 us (1%)
    unnamed x1, blocking collectives  249 us
    psum x1, waiting for transfers between devices, per_device(): lax.psum((part_in, part_out, part_gate), ('item', 'dp'))  181 us
    psum x1, blocking collectives, per_device(): totals_all = lax.psum(totals, 'item')  127 us
    psum x1, blocking collectives, per_device(): lax.psum((part_in, part_out, part_gate), ('item', 'dp'))  71.8 us
    all_gather x1, blocking collectives, per_device(): lax.all_gather(query_gate, 'item', axis=0, tiled=True)  44.4 us
    dot_general x8, matrix products, one_block(): jnp.einsum('kri,ikd->rkd', coef_bf, item_part, preferred_element_type=jnp...  41.9 us
    dot_general x8, matrix products, one_block(): jnp.einsum('rkd,ikd->kri', query_rows, item_part, preferred_element_type=...  32.5 us
    reduce_sum x8, other arithmetic, one_block(): jnp.sum(exp_logit[None] * weights * (score_matrix - TAU * logits[None]),...  23.9 us
  transfers between devices with their start and end apart: 3, of which 1 were waited for; matrix products, arithmetic and copies ran while one was open for 5% of the time, Pallas kernels for 0%

profile of v1, /device:TPU:2, one launch (start us, length us, event | category | flops | bytes accessed | tf_op | source)
XLA Modules:
  0.0 877.7 jit_solution(17275643459601341978)
XLA Ops:
  12.5 12.1 %all-to-all-start = ((bf16[64,16,256]{2,1,0:T(8,128)(2,1)}), bf16[64,16,256]{2,1,0:T(8,128)(2,1)S(1)}, u32[]{:S(2)}, u32[]{:S(2)}) async-start(bf16[64,16,256]{2,1,0:T(8,128)(2,1)} %stack.3), calls=%async_computation | async-start | bytes 1048576 | tf_op jit(solution)/shard_map/all_to_all | solution.py:98
  32.5 7.0 copy.73
  39.4 5.7 gather_fusion.1
  46.0 44.4 %all-gather = bf16[64,16,4]{1,2,0:T(4,128)(2,1)S(1)} all-gather(bf16[1,16,4]{1,2,0:T(4,128)(2,1)S(1)} %fusion.19), channel_id=1, replica_groups=mesh['item'=64,'dp'=4] {'item'}, dimensions={0}, use_global_device_ids=true | all-gather | bytes 8320 | tf_op jit(solution)/shard_map/all_gather | solution.py:100
  97.4 6.0 copy.80
  108.2 118.6 %while.17 = (s32[]{:T(128)}, f32[1024]{0:T(1024)S(1)}, f32[1024,4,64]{0,2,1:T(8,128)}, f32[4,1024]{1,0:T(4,128)S(1)}, f32[4,1024,1]{1,0,2:T(4,128)S(1)}, /*index...) while((s32[]{:T(128)}, f32[1024]{0:T(1024)S(1)}, ...), condition=%wide.region_7.8_spmd.clone, body=%wide.region_2.7_spmd.clone.sunk | while | flops 573056000 | bytes 49480844 | solution.py:56
  110.5 4.1 fusion.63
  117.9 5.0 fusion.64
  125.1 4.1 fusion.63
  132.5 5.3 fusion.64
  147.3 5.3 fusion.64
  154.7 4.1 fusion.63
  162.2 5.3 fusion.64
  169.6 4.1 fusion.63
  177.0 5.3 fusion.64
  184.4 4.1 fusion.63
  191.8 5.3 fusion.64
  206.7 5.3 fusion.64
  214.1 4.1 fusion.63
  221.5 5.3 fusion.64
  226.8 126.8 %psum.28 = f32[1024]{0:T(1024)S(1)} all-reduce(f32[1024]{0:T(1024)S(1)} %get-tuple-element.108), channel_id=1, replica_groups=mesh['item'=64,'dp'=4] {'item'}, use_global_device_ids=true, to_apply=%region_8.9 | all-reduce | flops 1024 | bytes 8192 | tf_op jit(solution)/shard_map/psum | solution.py:116
  358.9 249.2 %all-reduce = f32[1024,4]{1,0:T(8,128)S(1)} all-reduce(f32[1024,4]{1,0:T(8,128)S(1)} %copy.77), channel_id=3, replica_groups=mesh['item'=64,'dp'=4] {'item'}, use_global_device_ids=true, to_apply=%region_14.15.clone | all-reduce | flops 4096 | bytes 32768
  613.2 71.8 %psum.31 = f32[512,4]{0,1:T(4,128)} all-reduce(f32[512,4]{0,1:T(4,128)S(1)} %fusion.30), channel_id=1, replica_groups=mesh['item'=64,'dp'=4] {'item','dp'}, use_global_device_ids=true, to_apply=%region_17.18 | all-reduce | flops 2048 | bytes 16384 | tf_op jit(solution)/shard_map/psum | solution.py:143
  685.9 181.0 %all-reduce.4.cloned.1.call-done = (f32[256,512]{0,1:T(8,128)}, f32[512,256]{1,0:T(8,128)}) async-done(((f32[256,512]{0,1:T(8,128)}, f32[512,256]{1,0:T(8,128)}), (f32[256,512]{0,1:T(8,128)}, f32[512,256]{1,0:T(8,128)})) %all-reduce.4.cloned.1.call-update) | async-done | bytes 1048592 | tf_op jit(solution)/shard_map/psum | solution.py:143
  (166 shorter events, 91.8 us)
Async XLA Ops:
  10.7 14.0 %copy-start.3 = (f32[16,256]{1,0:T(8,128)}, f32[16,256]{1,0:T(8,128)S(1)}, u32[]{:S(2)}) copy-start(f32[16,256]{1,0:T(8,128)S(1)} %get-tuple-element.228) | copy-start | bytes 49156
  11.6 13.0 %copy-start.7 = (f32[16,256]{1,0:T(8,128)}, f32[16,256]{1,0:T(8,128)S(1)}, u32[]{:S(2)}) copy-start(f32[16,256]{1,0:T(8,128)S(1)} %mul.188) | copy-start | bytes 49156
  12.5 94.4 %all-to-all-start = ((bf16[64,16,256]{2,1,0:T(8,128)(2,1)}), bf16[64,16,256]{2,1,0:T(8,128)(2,1)S(1)}, u32[]{:S(2)}, u32[]{:S(2)}) async-start(bf16[64,16,256]{2,1,0:T(8,128)(2,1)} %stack.3), calls=%async_computation | async-start | bytes 1048576 | tf_op jit(solution)/shard_map/all_to_all | solution.py:98
  24.6 583.6 %reduce-scatter.2.cloned.1.call-start = ((), (), s32[]{:S(2)}) async-start(), calls=%async_computation.2 | async-start | bytes 1064960 | tf_op jit(solution)/shard_map/reduce_scatter | solution.py:120
  32.4 7.0 copy-start.12
  32.5 13.4 %copy-start.15 = (bf16[512,4]{0,1:T(4,128)(2,1)S(1)}, bf16[512,4]{0,1:T(4,128)(2,1)}, u32[]{:S(2)}) copy-start(bf16[512,4]{0,1:T(4,128)(2,1)} %param.17) | copy-start | bytes 12292
  97.4 8.9 %copy-start.5 = (f32[1024,4]{0,1:T(4,128)}, f32[1024,4]{0,1:T(4,128)S(1)}, u32[]{:S(2)}) copy-start(f32[1024,4]{0,1:T(4,128)S(1)} %copy.72) | copy-start | bytes 49156
  108.2 245.4 %copy-start.6 = (f32[1024,4]{0,1:T(4,128)S(1)}, f32[1024,4]{0,1:T(4,128)}, u32[]{:S(2)}) copy-start(f32[1024,4]{0,1:T(4,128)} %copy-done.5) | copy-start | bytes 49156
  110.5 4.4 copy-start.1
  125.1 4.4 copy-start.1
  154.7 4.4 copy-start.1
  169.6 4.4 copy-start.1
  184.4 4.4 copy-start.1
  199.2 4.4 copy-start.1
  214.0 4.4 copy-start.1
  226.8 130.5 %copy-start.11 = (f32[16,4]{1,0:T(8,128)S(1)}, f32[16,4]{1,0:T(8,128)}, u32[]{:S(2)}) copy-start(f32[16,4]{1,0:T(8,128)} %get-tuple-element.223) | copy-start | bytes 772
  226.8 130.7 %copy-start.17 = (u32[256]{0:T(256)S(1)}, u32[256]{0:T(256)}, u32[]{:S(2)}) copy-start(u32[256]{0:T(256)} %constant.108) | copy-start | bytes 3076
  226.8 381.4 %copy-start.4 = (f32[16,256]{1,0:T(8,128)S(1)}, f32[16,256]{1,0:T(8,128)}, u32[]{:S(2)}) copy-start(f32[16,256]{1,0:T(8,128)} %copy-done.3) | copy-start | bytes 49156
  226.8 382.5 %copy-start.8 = (f32[16,256]{1,0:T(8,128)S(1)}, f32[16,256]{1,0:T(8,128)}, u32[]{:S(2)}) copy-start(f32[16,256]{1,0:T(8,128)} %copy-done.7) | copy-start | bytes 49156
  226.8 383.2 %copy-start.2 = (bf16[512,256]{1,0:T(8,128)(2,1)S(1)}, bf16[512,256]{1,0:T(8,128)(2,1)}, u32[]{:S(2)}) copy-start(bf16[512,256]{1,0:T(8,128)(2,1)} %param.16) | copy-start | bytes 786436
  354.3 257.2 %copy-start.10 = (f32[16,512]{1,0:T(8,128)S(1)}, f32[16,512]{1,0:T(8,128)}, u32[]{:S(2)}) copy-start(f32[16,512]{1,0:T(8,128)} %get-tuple-element.226) | copy-start | bytes 98308
  354.3 257.2 %copy-start.16 = (bf16[512,4]{0,1:T(4,128)(2,1)S(1)}, bf16[512,4]{0,1:T(4,128)(2,1)}, u32[]{:S(2)}) copy-start(bf16[512,4]{0,1:T(4,128)(2,1)} %param.17) | copy-start | bytes 12292
  354.3 257.4 %copy-start.9 = (bf16[1,16,256]{2,1,0:T(8,128)(2,1)S(1)}, bf16[1,16,256]{2,1,0:T(8,128)(2,1)}, u32[]{:S(2)}) copy-start(bf16[1,16,256]{2,1,0:T(8,128)(2,1)} %param.10) | copy-start | bytes 24580
  357.2 509.7 %all-reduce.4.cloned.1.call-start = ((), (), s32[]{:S(2)}) async-start(), calls=%async_computation.3 | async-start | bytes 2097152 | tf_op jit(solution)/shard_map/psum | solution.py:143
  (4 other events, 11.5 us)
Sparse Core Ops, SparseCore 0:
  357.3 136.9 reduce-scatter.1
  613.1 253.7 all-reduce.3
